TPU v7x, 32 devices: a whole 2x2x4 slice. The times are simulated.
32 devices in a mesh: groups: 1, leaf: 32 (over z, y, x, core).
Axes of the slice: x: 2, y: 2, z: 4, core: 2. Of those that a mesh axis runs over, the one named last changes fastest.
Arguments:
- embeddings: bfloat16 [768, 65536], P(None, ('groups', 'leaf')), may hold values from -4 to 4
- probes: bfloat16 [32, 65536], P(None, ('groups', 'leaf')), may hold values from -1.75 to 1.75
- order: int32 [32, 2048], P(('groups', 'leaf')), may hold values from 0 to 2047, each once within a row
- near_list: int32 [256, 7], P(('groups', 'leaf')), may hold values from 0 to 255, as said below
- near_count: int32 [32, 8], P(('groups', 'leaf')), may hold values from 1 to 7, 32 in all within a row
- skeleton: int32 [30, 64], P('groups'), may hold values from 0 to 65535, as said below
- core: float32 [30, 64, 64], P('groups'), may hold values from -8 to 8
Outputs:
- values: float32 [32, 65536], P(None, ('groups', 'leaf'))
Inputs may be any that keep to these rules, and one draw needn't show every extreme that they name: `near_list`: slot 0 of leaf t holds t; every slot of leaf t holds a leaf within 3 of t. `near_count`: each row sums to 32, and its largest entry is 7. `skeleton`: entry r of node n lies among the examples of node n, in the r-th of 64 equal parts of them. `order`: each row is a permutation.
All inputs are finite; a program needn't handle non-finite values.
Results may differ from a plain program's by a relative error of at most 0.0042.
Values may be sent and summed in bfloat16 or wider, within the bound.
No kernel may reach another device: no remote copies, remote signals or barrier semaphores. Data moves between devices by JAX's collectives and lax.ppermute only.
A program may use at most 128 MiB of HBM per device.

v0:
```python
import jax
import jax.numpy as jnp
from jax import lax
from jax.sharding import PartitionSpec as P

LEAF = 256
R = 64
LEVELS = 4
W = 3
NEAR = 7


def with_halo(block, sides, width):
    for axis, dim in sides:
        count = lax.axis_size(axis)
        forward = [(i, i + 1) for i in range(count - 1)]
        backward = [(target, source) for source, target in forward]
        low = lax.ppermute(
            lax.slice_in_dim(block, block.shape[dim] - width, None, axis=dim), axis, forward
        )
        high = lax.ppermute(lax.slice_in_dim(block, 0, width, axis=dim), axis, backward)
        block = jnp.concatenate([low, block, high], axis=dim)
    return block


def kernel_matrix(left_emb, left_norm, right_emb, right_norm):
    inner = lax.dot_general(
        left_emb, right_emb, (((0,), (0,)), ((), ())), preferred_element_type=jnp.float32
    )
    distance = left_norm[:, None] + right_norm[None, :] - 2.0 * inner
    return jnp.exp(-0.5 * distance).astype(jnp.bfloat16)


def leaf_kernels(source_emb, source_norm, target_emb, target_norm):
    inner = jnp.einsum("eia,eib->iab", source_emb, target_emb, preferred_element_type=jnp.float32)
    distance = source_norm[:, :, None] + target_norm[:, None, :] - 2.0 * inner
    return jnp.exp(-0.5 * distance).astype(jnp.bfloat16)


def column_norms(columns):
    return jnp.sum(jnp.square(columns.astype(jnp.float32)), axis=0)


def body(embeddings, probes, order, near_list, near_count, skeleton, core):
    axis_devices = lax.axis_size("leaf")
    tree_bits = axis_devices.bit_length() - 1
    position = lax.axis_index("leaf")
    width_e = embeddings.shape[0]
    dev_points = embeddings.shape[1]
    dev_leaves = dev_points // LEAF
    x_tree = probes[:, order[0]]
    probe_cols = x_tree.shape[0]
    norms = column_norms(embeddings)
    stacked = jnp.concatenate([embeddings, x_tree], axis=0)
    padded = with_halo(stacked, (("leaf", 1),), W * LEAF)
    pad_blocks = padded.reshape(padded.shape[0], dev_leaves + 2 * W, LEAF)
    pad_emb = pad_blocks[:width_e]
    pad_x = pad_blocks[width_e:]
    pad_norm = jnp.sum(jnp.square(pad_emb.astype(jnp.float32)), axis=0)
    own_emb = embeddings.reshape(width_e, dev_leaves, LEAF)
    own_norm = norms.reshape(dev_leaves, LEAF)
    local_pos = near_list - position * dev_leaves + W
    counts = near_count[0]
    near_sum = jnp.zeros((probe_cols, dev_leaves, LEAF), jnp.float32)
    for slot_id in range(NEAR):
        sources = local_pos[:, slot_id]
        kernel_vals = leaf_kernels(
            jnp.take(pad_emb, sources, axis=1),
            jnp.take(pad_norm, sources, axis=0),
            own_emb,
            own_norm,
        )
        terms = jnp.einsum(
            "pia,iab->pib",
            jnp.take(pad_x, sources, axis=1),
            kernel_vals,
            preferred_element_type=jnp.float32,
        )
        near_sum = near_sum + jnp.where((slot_id < counts)[None, :, None], terms, 0.0)
    level_bits = [tree_bits - 1 - level_id for level_id in range(LEVELS)]
    own_nodes = [
        2 ** (level_id + 1) - 2 + jnp.right_shift(position, level_bits[level_id])
        for level_id in range(LEVELS)
    ]
    partner_nodes = [
        2 ** (level_id + 1)
        - 2
        + jnp.bitwise_xor(jnp.right_shift(position, level_bits[level_id]), 1)
        for level_id in range(LEVELS)
    ]
    start_point = position * dev_points
    slot_counts = [R * 2 ** (level_id + 1) // axis_devices for level_id in range(LEVELS)]
    slot_starts = [sum(slot_counts[:level_id]) for level_id in range(LEVELS)]
    picks = []
    for level_id in range(LEVELS):
        node_row = lax.dynamic_index_in_dim(skeleton, own_nodes[level_id], 0, keepdims=False)
        within = jnp.bitwise_and(position, (1 << level_bits[level_id]) - 1)
        point_ids = lax.dynamic_slice_in_dim(
            node_row, within * slot_counts[level_id], slot_counts[level_id]
        )
        picks.append(jnp.take(embeddings, point_ids - start_point, axis=1))
    owned = jnp.concatenate(picks, axis=1)
    gathered = lax.all_gather(owned, "leaf", axis=1, tiled=True)
    gathered = gathered.reshape(width_e, axis_devices, owned.shape[1])
    own_parts = []
    part_parts = []
    for level_id in range(LEVELS):
        first_node = 2 ** (level_id + 1) - 2
        level_cols = gathered[
            :, :, slot_starts[level_id] : slot_starts[level_id] + slot_counts[level_id]
        ]
        level_cols = level_cols.reshape(width_e, axis_devices * slot_counts[level_id])
        own_parts.append(
            lax.dynamic_slice_in_dim(level_cols, (own_nodes[level_id] - first_node) * R, R, axis=1)
        )
        part_parts.append(
            lax.dynamic_slice_in_dim(
                level_cols, (partner_nodes[level_id] - first_node) * R, R, axis=1
            )
        )
    own_cols = jnp.concatenate(own_parts, axis=1)
    part_cols = jnp.concatenate(part_parts, axis=1)
    own_sums = jnp.dot(
        x_tree,
        kernel_matrix(embeddings, norms, own_cols, column_norms(own_cols)),
        preferred_element_type=jnp.float32,
    )
    node_terms = jnp.zeros((probe_cols, skeleton.shape[0] * R), jnp.float32)
    for level_id in range(LEVELS):
        node_terms = lax.dynamic_update_slice_in_dim(
            node_terms,
            own_sums[:, level_id * R : (level_id + 1) * R],
            own_nodes[level_id] * R,
            axis=1,
        )
    node_totals = lax.psum(node_terms, "leaf")
    partner_sums = [
        lax.dynamic_slice_in_dim(node_totals, partner_nodes[level_id] * R, R, axis=1)
        for level_id in range(LEVELS)
    ]
    weights = []
    for level_id in range(LEVELS):
        core_part = lax.dynamic_index_in_dim(core, partner_nodes[level_id], 0, keepdims=False)
        weights.append(
            jnp.dot(partner_sums[level_id], core_part, precision=lax.Precision.HIGHEST).astype(
                jnp.bfloat16
            )
        )
    far_kernel = kernel_matrix(part_cols, column_norms(part_cols), embeddings, norms)
    far_sum = jnp.dot(
        jnp.concatenate(weights, axis=1), far_kernel, preferred_element_type=jnp.float32
    )
    tree_values = near_sum.reshape(probe_cols, dev_points) + far_sum
    return jnp.zeros_like(tree_values).at[:, order[0]].set(tree_values)


def solution(mesh):
    return jax.shard_map(
        body,
        mesh=mesh,
        in_specs=(
            P(None, ("groups", "leaf")),
            P(None, ("groups", "leaf")),
            P(("groups", "leaf"), None),
            P(("groups", "leaf"), None),
            P(("groups", "leaf"), None),
            P("groups", None),
            P("groups", None, None),
        ),
        out_specs=P(None, ("groups", "leaf")),
        check_vma=False,
    )
```

profile of v0, /device:TPU:0, one launch (start us, length us, event | category | flops | bytes accessed | tf_op | source)
XLA Modules:
  0.0 336.7 jit_solution(11105078149921155437)
XLA Ops:
  6.5 0.9 compare_and_fusion.8
  7.4 0.8 compare_and_fusion.7
  8.2 0.8 compare_and_fusion.10
  9.0 0.7 subtract_add_fusion
  10.0 0.8 compare_and_fusion.9
  10.7 4.6 %copy.41 = bf16[768,2048]{0,1:T(8,128)(2,1)} copy(bf16[768,2048]{1,0:T(8,128)(2,1)} %param.13) | data formatting | bytes 6291456 | tf_op args[0]
  15.4 2.9 gather_fusion.1
  18.3 2.9 gather_fusion.2
  21.2 2.9 gather_fusion.3
  24.1 2.9 gather_fusion.4
  27.3 0.7 maximum_bitcast_fusion
  28.4 6.2 %gather_fusion = bf16[2048,32]{1,0:T(8,128)(2,1)S(1)} fusion(bf16[32,2048]{0,1:T(8,128)(2,1)S(1)} %copy.40, s32[2048]{0:T(1024)S(1)} %broadcast_clamp_fusion), kind=kCustom, calls=%fused_computation.21 | custom fusion | bytes 270336 | tf_op jit(solution)/shard_map/gather | solution.py:51
  34.6 3.0 pad_maximum_fusion.4
  37.6 2.5 copy.43
  40.1 1.4 collective-permute-start.1
  41.5 1.5 copy.42
  43.0 4.2 %collective-permute-start = (bf16[800,768]{1,0:T(8,128)(2,1)}, bf16[800,768]{1,0:T(8,128)(2,1)}, u32[]{:S(2)}, u32[]{:S(2)}) collective-permute-start(bf16[800,768]{1,0:T(8,128)(2,1)} %copy.42), channel_id=1, source_target_pairs={{0,1},{1,2},{2,3},{3,4},{4,5},{5,6},{6,7},{7,8},{8,9},{9,10},{10,1... | collective-permute-start | bytes 3686408 | tf_op jit(solution)/shard_map/ppermute | solution.py:18
  47.2 2.6 multiply_reduce_fusion.1
  50.1 1.8 copy.45
  51.9 2.5 copy.44
  54.3 6.6 %multiply_reduce_fusion = (f32[3584]{0:T(1024)S(1)}, bf16[768,3584]{0,1:T(8,128)(2,1)}) fusion(bf16[800,768]{0,1:T(8,128)(2,1)S(1)} %copy.45, bf16[32,2048]{0,1:T(8,128)(2,1)S(1)} %bitcast.279, bf16[768,2048]{0,1:T(8,128)(2,1)} %copy.41, bf16[800,768]{0,1:T(8,128)(2,1)} %copy.44), kind=kLoop, calls=%fused_computation.27 | loop fusion | flops 30274048 | bytes 11253760 | tf_op jit(solution)/shard_map/reduce_sum | solution.py:59
  61.0 2.1 pad_maximum_fusion.5
  63.1 1.5 copy.50
  64.6 0.6 gather_fusion.23
  65.1 0.6 gather_fusion.20
  65.7 0.6 gather_fusion.25
  66.8 0.6 gather_fusion.17
  67.9 0.6 gather_fusion.14
  69.1 0.6 gather_fusion.11
  69.6 0.6 gather_fusion.13
  70.2 0.6 gather_fusion.8
  71.3 0.6 gather_fusion.5
  72.5 8.2 %copy.46 = bf16[768,14,256]{2,0,1:T(8,128)(2,1)} copy(bf16[768,14,256]{0,2,1:T(8,128)(2,1)} %bitcast.269) | data formatting | bytes 11010048 | tf_op jit(solution)/shard_map/slice | solution.py:57
  80.7 5.1 %gather_fusion.6 = bf16[8,768,256]{2,1,0:T(8,128)(2,1)} fusion(bf16[768,14,256]{2,0,1:T(8,128)(2,1)} %copy.46, s32[1024]{0:T(1024)S(1)} %pad_clamp_fusion.10), kind=kCustom, calls=%fused_computation.1.clone | custom fusion | bytes 6291488 | tf_op jit(solution)/shard_map/jit(_take)/gather | solution.py:68
  85.7 5.0 %gather_fusion.9 = bf16[8,768,256]{2,1,0:T(8,128)(2,1)} fusion(bf16[768,14,256]{2,0,1:T(8,128)(2,1)} %copy.46, s32[1024]{0:T(1024)S(1)} %pad_clamp_fusion.9), kind=kCustom, calls=%fused_computation.9.clone | custom fusion | bytes 6291488 | tf_op jit(solution)/shard_map/jit(_take)/gather | solution.py:68
  90.7 5.0 %gather_fusion.12 = bf16[8,768,256]{2,1,0:T(8,128)(2,1)} fusion(bf16[768,14,256]{2,0,1:T(8,128)(2,1)} %copy.46, s32[1024]{0:T(1024)S(1)} %pad_clamp_fusion.8), kind=kCustom, calls=%fused_computation.10.clone | custom fusion | bytes 6291488 | tf_op jit(solution)/shard_map/jit(_take)/gather | solution.py:68
  95.6 5.0 %gather_fusion.15 = bf16[8,768,256]{2,1,0:T(8,128)(2,1)} fusion(bf16[768,14,256]{2,0,1:T(8,128)(2,1)} %copy.46, s32[1024]{0:T(1024)S(1)} %pad_clamp_fusion.7), kind=kCustom, calls=%fused_computation.11.clone | custom fusion | bytes 6291488 | tf_op jit(solution)/shard_map/jit(_take)/gather | solution.py:68
  100.6 5.0 %gather_fusion.18 = bf16[8,768,256]{2,1,0:T(8,128)(2,1)} fusion(bf16[768,14,256]{2,0,1:T(8,128)(2,1)} %copy.46, s32[1024]{0:T(1024)S(1)} %pad_clamp_fusion.6), kind=kCustom, calls=%fused_computation.12.clone | custom fusion | bytes 6291488 | tf_op jit(solution)/shard_map/jit(_take)/gather | solution.py:68
  105.7 5.1 %gather_fusion.21 = bf16[8,768,256]{2,1,0:T(8,128)(2,1)} fusion(bf16[768,14,256]{2,0,1:T(8,128)(2,1)} %copy.46, s32[1024]{0:T(1024)S(1)} %pad_clamp_fusion.5), kind=kCustom, calls=%fused_computation.13.clone | custom fusion | bytes 6291488 | tf_op jit(solution)/shard_map/jit(_take)/gather | solution.py:68
  110.8 5.0 %gather_fusion.24 = bf16[8,768,256]{2,1,0:T(8,128)(2,1)} fusion(bf16[768,14,256]{2,0,1:T(8,128)(2,1)} %copy.46, s32[1024]{0:T(1024)S(1)} %pad_clamp_fusion.4), kind=kCustom, calls=%fused_computation.14.clone | custom fusion | bytes 6291488 | tf_op jit(solution)/shard_map/jit(_take)/gather | solution.py:68
  116.2 3.9 %fusion.181 = f32[8,256,32]{1,2,0:T(8,128)S(1)} fusion(bf16[8,768,256]{2,1,0:T(8,128)(2,1)} %gather_fusion.6, pred[8]{0:T(512)(128)(4,1)S(1)} %get-tuple-element.58, f32[8,256]{1,0:T(8,128)S(1)} %add.373, f32[8,256]{1,0:T(8,128)S(1)} %broadcast_select_fusion.6, bf16[96,8,8,256]{3,2,1,0:T(8,128)(2,1)} %bitcast.270, ...), kind=kOutput, calls=%fused_computation.117 | convolution fusion | flops 843186176 | bytes 6701072 | tf_op jit(solution)/shard_map/pia,iab->pib/dot_general | solution.py:73
  120.1 3.9 %fusion.176 = f32[8,256,32]{1,2,0:T(8,128)S(1)} fusion(f32[8,256,32]{1,2,0:T(8,128)S(1)} %fusion.181, bf16[8,768,256]{2,1,0:T(8,128)(2,1)} %gather_fusion.9, pred[8]{0:T(512)(128)(4,1)S(1)} %get-tuple-element.57, f32[8,256]{1,0:T(8,128)S(1)} %broadcast_select_fusion.5, f32[8,256]{1,0:T(8,128)S(1)} %add.373, bf16[96,8,8,256]{3,2,1,0:T(8,128)(2,1)} %bitcast.271, ...), kind=kOutput, calls=%fused_computation.116 | convolution fusion | flops 843251712 | bytes 6963216 | tf_op jit(solution)/shard_map/pia,iab->pib/dot_general | solution.py:73
  124.0 3.9 %fusion.166 = f32[8,256,32]{1,2,0:T(8,128)S(1)} fusion(f32[8,256,32]{1,2,0:T(8,128)S(1)} %fusion.176, bf16[8,768,256]{2,1,0:T(8,128)(2,1)} %gather_fusion.12, pred[8]{0:T(512)(128)(4,1)S(1)} %get-tuple-element.56, f32[8,256]{1,0:T(8,128)S(1)} %broadcast_select_fusion.4, f32[8,256]{1,0:T(8,128)S(1)} %add.373, bf16[96,8,8,256]{3,2,1,0:T(8,128)(2,1)} %bitcast.272, ...), kind=kOutput, calls=%fused_computation.114 | convolution fusion | flops 843251712 | bytes 6963216 | tf_op jit(solution)/shard_map/pia,iab->pib/dot_general | solution.py:73
  127.9 3.9 %fusion.156 = f32[8,256,32]{1,2,0:T(8,128)S(1)} fusion(f32[8,256,32]{1,2,0:T(8,128)S(1)} %fusion.166, bf16[8,768,256]{2,1,0:T(8,128)(2,1)} %gather_fusion.15, pred[8]{0:T(512)(128)(4,1)S(1)} %get-tuple-element.55, f32[8,256]{1,0:T(8,128)S(1)} %broadcast_select_fusion.3, f32[8,256]{1,0:T(8,128)S(1)} %add.373, bf16[96,8,8,256]{3,2,1,0:T(8,128)(2,1)} %bitcast.273, ...), kind=kOutput, calls=%fused_computation.112 | convolution fusion | flops 843251712 | bytes 6963216 | tf_op jit(solution)/shard_map/pia,iab->pib/dot_general | solution.py:73
  131.8 3.9 %fusion.146 = f32[8,256,32]{1,2,0:T(8,128)S(1)} fusion(f32[8,256,32]{1,2,0:T(8,128)S(1)} %fusion.156, bf16[8,768,256]{2,1,0:T(8,128)(2,1)} %gather_fusion.18, pred[8]{0:T(512)(128)(4,1)S(1)} %get-tuple-element.54, f32[8,256]{1,0:T(8,128)S(1)} %broadcast_select_fusion.2, f32[8,256]{1,0:T(8,128)S(1)} %add.373, bf16[96,8,8,256]{3,2,1,0:T(8,128)(2,1)} %bitcast.274, ...), kind=kOutput, calls=%fused_computation.110 | convolution fusion | flops 843251712 | bytes 6963216 | tf_op jit(solution)/shard_map/pia,iab->pib/dot_general | solution.py:73
  135.7 5.2 %fusion.136 = f32[8,256,32]{1,2,0:T(8,128)} fusion(f32[8,256,32]{1,2,0:T(8,128)S(1)} %fusion.146, bf16[8,768,256]{2,1,0:T(8,128)(2,1)} %gather_fusion.21, pred[8]{0:T(512)(128)(4,1)S(1)} %get-tuple-element.53, f32[8,256]{1,0:T(8,128)S(1)} %broadcast_select_fusion.1, f32[8,256]{1,0:T(8,128)S(1)} %add.373, bf16[96,8,8,256]{3,2,1,0:T(8,128)(2,1)} %bitcast.275, ...), kind=kOutput, calls=%fused_computation.108 | convolution fusion | flops 843251712 | bytes 6963216 | tf_op jit(solution)/shard_map/pia,iab->pib/dot_general | solution.py:73
  140.9 5.3 %reshape.494 = bf16[1920,768]{1,0:T(8,128)(2,1)} reshape(bf16[32,60,768]{2,1,0:T(8,128)(2,1)} %all-gather.3.cloned.1.call-done) | data formatting | bytes 5898240
  146.2 5.3 %reshape.251 = bf16[768,32,60]{0,2,1:T(8,128)(2,1)} reshape(bf16[768,1920]{0,1:T(8,128)(2,1)} %bitcast.277) | data formatting | bytes 5898240 | tf_op jit(solution)/shard_map/reshape | solution.py:104
  151.5 1.0 slice.136
  152.6 1.3 slice_bitcast_fusion
  153.8 1.5 slice.138
  155.4 3.4 %slice.139 = bf16[768,32,32]{0,2,1:T(8,128)(2,1)} slice(bf16[768,32,60]{0,2,1:T(8,128)(2,1)} %reshape.251), slice={[0:768], [0:32], [28:60]} | slice | bytes 3145728 | tf_op jit(solution)/shard_map/slice | solution.py:109
  158.9 1.0 constant_dynamic-slice_fusion.4
  160.1 3.3 fusion.52
  165.0 0.7 copy-done.1
  165.7 3.9 %fusion.126 = f32[8,4,8,256]{3,2,1,0:T(8,128)S(1)} fusion(f32[8,256,32]{1,2,0:T(8,128)S(1)} %copy-done.5, bf16[8,768,256]{2,1,0:T(8,128)(2,1)} %gather_fusion.24, pred[8]{0:T(512)(128)(4,1)S(1)} %get-tuple-element.52, f32[8,256]{1,0:T(8,128)S(1)} %broadcast_select_fusion, f32[8,256]{1,0:T(8,128)S(1)} %add.373, bf16[96,8,8,256]{3,2,1,0:T(8,128)(2,1)} %bitcast.276, ...), kind=kOutput, calls=%fused_computation.106 | convolution fusion | flops 843251712 | bytes 6963216 | tf_op jit(solution)/shard_map/pia,iab->pib/dot_general | solution.py:73
  169.8 145.9 %all-reduce.2.cloned.1.call-done = f32[32,1920]{1,0:T(8,128)} async-done(((f32[32,1920]{1,0:T(8,128)}), f32[32,1920]{1,0:T(8,128)}) %all-reduce.2.cloned.1.call-update) | async-done | bytes 245776 | tf_op jit(solution)/shard_map/psum | solution.py:136
  315.7 0.9 convolution_convert_fusion
  316.6 0.9 convolution_convert_fusion.1
  317.6 0.9 convolution_convert_fusion.2
  318.5 0.9 convolution_convert_fusion.3
  319.4 3.2 fusion.44
  323.0 5.8 %scatter_custom_fusion = f32[32,2048]{0,1:T(8,128)S(1)} fusion(s32[2048]{0:T(1024)S(1)} %bitcast.286, f32[2048,32]{1,0:T(8,128)S(1)} %copy.80, f32[]{:T(128)} %constant.201.clone.1), kind=kCustom, calls=%fused_computation.168 | custom fusion | bytes 262148 | tf_op jit(solution)/shard_map/scatter | solution.py:154
  328.9 1.0 copy.81
  (77 shorter events, 6.7 us)
Async XLA Ops:
  6.5 309.1 %copy-start = (f32[30,64,64]{2,1,0:T(8,128)S(1)}, f32[30,64,64]{2,1,0:T(8,128)}, u32[]{:S(2)}) copy-start(f32[30,64,64]{2,1,0:T(8,128)} %param.19) | copy-start | bytes 1474564
  6.5 134.4 %all-gather.3.cloned.1.call-start = ((), (), s32[]{:S(2)}) async-start(), calls=%async_computation.1 | async-start | bytes 3244032 | tf_op jit(solution)/shard_map/all_gather | solution.py:103
  18.2 9.8 %copy-start.3 = (s32[1,2048]{1,0:T(1,128)S(1)}, s32[1,2048]{1,0:T(1,128)}, u32[]{:S(2)}) copy-start(s32[1,2048]{1,0:T(1,128)} %param.15) | copy-start | bytes 24580
  18.3 9.9 %copy-start.2 = (bf16[32,2048]{1,0:T(8,128)(2,1)S(1)}, bf16[32,2048]{1,0:T(8,128)(2,1)}, u32[]{:S(2)}) copy-start(bf16[32,2048]{1,0:T(8,128)(2,1)} %param.14) | copy-start | bytes 393220
  28.0 287.6 %all-reduce.2.cloned.1.call-start = ((), (), s32[]{:S(2)}) async-start(), calls=%async_computation | async-start | bytes 491520 | tf_op jit(solution)/shard_map/psum | solution.py:136
  40.1 9.9 %copy-start.4 = (s32[1,8]{1,0:T(1,128)S(1)}, s32[1,8]{1,0:T(1,128)}, u32[]{:S(2)}) copy-start(s32[1,8]{1,0:T(1,128)} %param.17) | copy-start | bytes 100
  40.1 10.0 %collective-permute-start.1 = (bf16[800,768]{1,0:T(8,128)(2,1)}, bf16[800,768]{1,0:T(8,128)(2,1)}, u32[]{:S(2)}, u32[]{:S(2)}) collective-permute-start(bf16[800,768]{1,0:T(8,128)(2,1)} %copy.43), channel_id=1, source_target_pairs={{1,0},{2,1},{3,2},{4,3},{5,4},{6,5},{7,6},{8,7},{9,8},{10,9},{11,1... | collective-permute-start | bytes 3686408 | tf_op jit(solution)/shard_map/ppermute | solution.py:21
  43.0 8.8 %collective-permute-start = (bf16[800,768]{1,0:T(8,128)(2,1)}, bf16[800,768]{1,0:T(8,128)(2,1)}, u32[]{:S(2)}, u32[]{:S(2)}) collective-permute-start(bf16[800,768]{1,0:T(8,128)(2,1)} %copy.42), channel_id=1, source_target_pairs={{0,1},{1,2},{2,3},{3,4},{4,5},{5,6},{6,7},{7,8},{8,9},{9,10},{10,1... | collective-permute-start | bytes 3686408 | tf_op jit(solution)/shard_map/ppermute | solution.py:18
  160.1 5.6 %copy-start.5 = (f32[8,256,32]{1,2,0:T(8,128)S(1)}, f32[8,256,32]{1,2,0:T(8,128)}, u32[]{:S(2)}) copy-start(f32[8,256,32]{1,2,0:T(8,128)} %fusion.136) | copy-start | bytes 786436
  165.0 0.7 copy-start.1
Sparse Core Ops, SparseCore 0:
  28.2 68.4 all-gather.2
  165.8 149.8 all-reduce.1
where the time goes:
time: 339 us; the launch traced here: 337 us
  waiting for transfers between devices  146 us (43%)
  local copies, waits for them, and re-layouts  112 us (33%)
  matrix products  38.8 us (11%)
  other arithmetic  20.1 us (6%)
  between operations  14 us (4%)
  starting transfers between devices  5.62 us (2%)
    psum x1, waiting for transfers between devices, body(): node_totals = lax.psum(node_terms, 'leaf')  146 us
    gather x7, local copies, waits for them, and re-layouts, body(): jnp.take(pad_emb, sources, axis=1)  35.1 us
    dot_general x7, matrix products, body(): jnp.einsum('pia,iab->pib', jnp.take(pad_x, sources, axis=1), kernel_vals,...  28.6 us
    gather x4, local copies, waits for them, and re-layouts, body(): picks.append(jnp.take(embeddings, point_ids - start_point, axis=1))  11.6 us
    unnamed x15, local copies, waits for them, and re-layouts  10.9 us
    slice x1, local copies, waits for them, and re-layouts, body(): pad_emb = pad_blocks[:width_e]  8.19 us
    scatter x2, local copies, waits for them, and re-layouts, body(): return jnp.zeros_like(tree_values).at[:, order[0]].set(tree_values)  6.86 us
  transfers between devices with their start and end apart: 4, of which 1 were waited for; matrix products, arithmetic and copies ran while one was open for 33% of the time, Pallas kernels for 0%

commit v1 on v0

--- a/solution.py
+++ b/solution.py
@@ -133,7 +133,7 @@
             own_nodes[level_id] * R,
             axis=1,
         )
-    node_totals = lax.psum(node_terms, "leaf")
+    node_totals = jnp.sum(lax.all_gather(node_terms, "leaf"), axis=0)
     partner_sums = [
         lax.dynamic_slice_in_dim(node_totals, partner_nodes[level_id] * R, R, axis=1)
         for level_id in range(LEVELS)

time: 339 us -> 277 us (0.82)
  the two profiles are of different devices: /device:TPU:0 before, /device:TPU:13 now
where the time goes in v1:
time: 277 us; the launch traced here: 275 us
  local copies, waits for them, and re-layouts  113 us (41%)
  waiting for transfers between devices  83.4 us (30%)
  matrix products  34.9 us (13%)
  other arithmetic  24.1 us (9%)
  between operations  14.2 us (5%)
  starting transfers between devices  5.77 us (2%)
    all_gather x1, waiting for transfers between devices, body(): gathered = lax.all_gather(owned, 'leaf', axis=1, tiled=True)  50.5 us
    gather x7, local copies, waits for them, and re-layouts, body(): jnp.take(pad_emb, sources, axis=1)  34.9 us
    ppermute x1, waiting for transfers between devices, with_halo(): lax.ppermute(lax.slice_in_dim(block, 0, width, axis=dim), axis, backward)  32.9 us
    dot_general x7, matrix products, body(): jnp.einsum('pia,iab->pib', jnp.take(pad_x, sources, axis=1), kernel_vals,...  27.5 us
    gather x4, local copies, waits for them, and re-layouts, body(): picks.append(jnp.take(embeddings, point_ids - start_point, axis=1))  11.6 us
    unnamed x23, local copies, waits for them, and re-layouts  11 us
    slice x1, local copies, waits for them, and re-layouts, body(): pad_emb = pad_blocks[:width_e]  8.29 us
    scatter x2, local copies, waits for them, and re-layouts, body(): return jnp.zeros_like(tree_values).at[:, order[0]].set(tree_values)  6.86 us
  transfers between devices with their start and end apart: 4, of which 2 were waited for; matrix products, arithmetic and copies ran while one was open for 40% of the time, Pallas kernels for 0%

profile of v1, /device:TPU:13, one launch (start us, length us, event | category | flops | bytes accessed | tf_op | source)
XLA Modules:
  0.0 275.3 jit_solution(9043692153368033709)
XLA Ops:
  6.5 0.9 compare_and_fusion.8
  7.4 0.8 compare_and_fusion.7
  8.2 0.8 compare_and_fusion.10
  9.0 0.7 subtract_add_fusion
  9.7 0.8 slice_reduce_fusion
  10.4 1.3 compare_and_fusion.9
  11.7 4.7 %copy.41 = bf16[768,2048]{0,1:T(8,128)(2,1)} copy(bf16[768,2048]{1,0:T(8,128)(2,1)} %param.13) | data formatting | bytes 6291456 | tf_op args[0]
  16.5 2.9 %gather_fusion.1 = bf16[4,768]{1,0:T(4,128)(2,1)S(1)} fusion(bf16[768,2048]{0,1:T(8,128)(2,1)} %copy.41, s32[1024]{0:T(1024)S(1)} %pad_clamp_fusion.3), kind=kCustom, calls=%fused_computation.22 | custom fusion | bytes 12304 | tf_op jit(solution)/shard_map/jit(_take)/gather | solution.py:101
  19.4 2.9 %gather_fusion.2 = bf16[8,768]{1,0:T(8,128)(2,1)S(1)} fusion(bf16[768,2048]{0,1:T(8,128)(2,1)} %copy.41, s32[1024]{0:T(1024)S(1)} %pad_clamp_fusion.2), kind=kCustom, calls=%fused_computation.23 | custom fusion | bytes 24608 | tf_op jit(solution)/shard_map/jit(_take)/gather | solution.py:101
  22.3 2.9 %gather_fusion.3 = bf16[16,768]{1,0:T(8,128)(2,1)S(1)} fusion(bf16[768,2048]{0,1:T(8,128)(2,1)} %copy.41, s32[1024]{0:T(1024)S(1)} %pad_clamp_fusion.1), kind=kCustom, calls=%fused_computation.24 | custom fusion | bytes 49216 | tf_op jit(solution)/shard_map/jit(_take)/gather | solution.py:101
  25.2 2.9 %gather_fusion.4 = bf16[32,768]{1,0:T(8,128)(2,1)S(1)} fusion(bf16[768,2048]{0,1:T(8,128)(2,1)} %copy.41, s32[1024]{0:T(1024)S(1)} %pad_clamp_fusion), kind=kCustom, calls=%fused_computation.25 | custom fusion | bytes 98432 | tf_op jit(solution)/shard_map/jit(_take)/gather | solution.py:101
  28.4 0.7 maximum_bitcast_fusion
  29.6 6.2 %gather_fusion = bf16[2048,32]{1,0:T(8,128)(2,1)S(1)} fusion(bf16[32,2048]{0,1:T(8,128)(2,1)S(1)} %copy.40, s32[2048]{0:T(1024)S(1)} %broadcast_clamp_fusion), kind=kCustom, calls=%fused_computation.21 | custom fusion | bytes 270336 | tf_op jit(solution)/shard_map/gather | solution.py:51
  35.8 2.6 multiply_reduce_fusion.1
  38.3 50.5 %all-gather.6.cloned.1.call-done = bf16[32,60,768]{2,1,0:T(8,128)(2,1)} async-done(((bf16[1,60,768]{2,1,0:T(8,128)(2,1)}), bf16[32,60,768]{2,1,0:T(8,128)(2,1)}) %all-gather.6.cloned.1.call-update) | async-done | bytes 2949136 | tf_op jit(solution)/shard_map/all_gather | solution.py:103
  88.8 5.3 %reshape.502 = bf16[1920,768]{1,0:T(8,128)(2,1)} reshape(bf16[32,60,768]{2,1,0:T(8,128)(2,1)} %all-gather.6.cloned.1.call-done) | data formatting | bytes 5898240
  94.1 5.3 %reshape.259 = bf16[768,32,60]{0,2,1:T(8,128)(2,1)} reshape(bf16[768,1920]{0,1:T(8,128)(2,1)} %bitcast.285) | data formatting | bytes 5898240 | tf_op jit(solution)/shard_map/reshape | solution.py:104
  99.4 1.0 slice.136
  100.5 1.3 slice_bitcast_fusion
  101.7 1.5 slice.138
  103.3 3.4 %slice.139 = bf16[768,32,32]{0,2,1:T(8,128)(2,1)} slice(bf16[768,32,60]{0,2,1:T(8,128)(2,1)} %reshape.259), slice={[0:768], [0:32], [28:60]} | slice | bytes 3145728 | tf_op jit(solution)/shard_map/slice | solution.py:109
  106.8 1.0 constant_dynamic-slice_fusion.4
  108.0 3.3 %fusion.52 = f32[32,256]{1,0:T(8,128)S(1)} fusion(bf16[2048,32]{1,0:T(8,128)(2,1)S(1)} %gather_fusion, bf16[768,2048]{1,0:T(8,128)(2,1)} %param.13, f32[256]{0:T(256)S(1)} %multiply_reduce_fusion.3, f32[2048]{0:T(1024)S(1)} %multiply_reduce_fusion.1, bf16[768,64]{0,1:T(8,128)(2,1)S(1)} %get-tuple-element.27, bf16[768,64]{0,1:T(8,128)(2,1)S(1)} %get-tuple-element.29, ...), kind=kOutput, calls=%fused_computation.96 | convolution fusion | flops 843055104 | bytes 3712000 | tf_op jit(solution)/shard_map/dot_general | solution.py:123
  113.0 0.7 copy-done.1
  113.7 2.9 %pad_maximum_fusion.4 = (bf16[800,768]{0,1:T(8,128)(2,1)S(1)}, bf16[800,768]{0,1:T(8,128)(2,1)}) fusion(bf16[32,2048]{0,1:T(8,128)(2,1)S(1)} %bitcast.286, bf16[768,2048]{0,1:T(8,128)(2,1)} %copy.41), kind=kLoop, calls=%fused_computation.95 | loop fusion | flops 4915200 | bytes 5734400 | tf_op jit(solution)/shard_map/slice | solution.py:19
  116.7 2.5 copy.43
  119.1 2.1 collective-permute-start.1
  121.3 1.5 copy.42
  122.8 3.6 %collective-permute-start = (bf16[800,768]{1,0:T(8,128)(2,1)}, bf16[800,768]{1,0:T(8,128)(2,1)}, u32[]{:S(2)}, u32[]{:S(2)}) collective-permute-start(bf16[800,768]{1,0:T(8,128)(2,1)} %copy.42), channel_id=1, source_target_pairs={{0,1},{1,2},{2,3},{3,4},{4,5},{5,6},{6,7},{7,8},{8,9},{9,10},{10,1... | collective-permute-start | bytes 3686408 | tf_op jit(solution)/shard_map/ppermute | solution.py:18
  126.7 32.9 %collective-permute-done.1 = bf16[800,768]{1,0:T(8,128)(2,1)} collective-permute-done((bf16[800,768]{1,0:T(8,128)(2,1)}, bf16[800,768]{1,0:T(8,128)(2,1)}, u32[]{:S(2)}, u32[]{:S(2)}) %collective-permute-start.1) | collective-permute-done | bytes 1228832 | tf_op jit(solution)/shard_map/ppermute | solution.py:21
  159.6 1.8 copy.45
  161.4 2.5 copy.44
  163.9 6.7 %multiply_reduce_fusion = (f32[3584]{0:T(1024)S(1)}, bf16[768,3584]{0,1:T(8,128)(2,1)}) fusion(bf16[800,768]{0,1:T(8,128)(2,1)S(1)} %copy.45, bf16[32,2048]{0,1:T(8,128)(2,1)S(1)} %bitcast.287, bf16[768,2048]{0,1:T(8,128)(2,1)} %copy.41, bf16[800,768]{0,1:T(8,128)(2,1)} %copy.44), kind=kLoop, calls=%fused_computation.27 | loop fusion | flops 30274048 | bytes 11253760 | tf_op jit(solution)/shard_map/reduce_sum | solution.py:59
  170.5 2.1 pad_maximum_fusion.5
  172.6 1.5 copy.50
  174.1 0.6 gather_fusion.23
  174.7 0.6 gather_fusion.20
  175.2 0.6 gather_fusion.25
  175.8 0.6 gather_fusion.22
  176.4 0.6 gather_fusion.17
  176.9 0.6 gather_fusion.19
  177.5 0.6 gather_fusion.14
  178.6 0.6 gather_fusion.11
  179.7 0.6 gather_fusion.8
  180.9 0.6 gather_fusion.5
  182.0 8.3 %copy.46 = bf16[768,14,256]{2,0,1:T(8,128)(2,1)} copy(bf16[768,14,256]{0,2,1:T(8,128)(2,1)} %bitcast.277) | data formatting | bytes 11010048 | tf_op jit(solution)/shard_map/slice | solution.py:57
  190.3 5.1 %gather_fusion.6 = bf16[8,768,256]{2,1,0:T(8,128)(2,1)} fusion(bf16[768,14,256]{2,0,1:T(8,128)(2,1)} %copy.46, s32[1024]{0:T(1024)S(1)} %pad_clamp_fusion.10), kind=kCustom, calls=%fused_computation.1.clone | custom fusion | bytes 6291488 | tf_op jit(solution)/shard_map/jit(_take)/gather | solution.py:68
  195.4 5.0 %gather_fusion.9 = bf16[8,768,256]{2,1,0:T(8,128)(2,1)} fusion(bf16[768,14,256]{2,0,1:T(8,128)(2,1)} %copy.46, s32[1024]{0:T(1024)S(1)} %pad_clamp_fusion.9), kind=kCustom, calls=%fused_computation.9.clone | custom fusion | bytes 6291488 | tf_op jit(solution)/shard_map/jit(_take)/gather | solution.py:68
  200.3 5.0 %gather_fusion.12 = bf16[8,768,256]{2,1,0:T(8,128)(2,1)} fusion(bf16[768,14,256]{2,0,1:T(8,128)(2,1)} %copy.46, s32[1024]{0:T(1024)S(1)} %pad_clamp_fusion.8), kind=kCustom, calls=%fused_computation.10.clone | custom fusion | bytes 6291488 | tf_op jit(solution)/shard_map/jit(_take)/gather | solution.py:68
  205.3 5.0 %gather_fusion.15 = bf16[8,768,256]{2,1,0:T(8,128)(2,1)} fusion(bf16[768,14,256]{2,0,1:T(8,128)(2,1)} %copy.46, s32[1024]{0:T(1024)S(1)} %pad_clamp_fusion.7), kind=kCustom, calls=%fused_computation.11.clone | custom fusion | bytes 6291488 | tf_op jit(solution)/shard_map/jit(_take)/gather | solution.py:68
  210.4 4.9 %gather_fusion.18 = bf16[8,768,256]{2,1,0:T(8,128)(2,1)} fusion(bf16[768,14,256]{2,0,1:T(8,128)(2,1)} %copy.46, s32[1024]{0:T(1024)S(1)} %pad_clamp_fusion.6), kind=kCustom, calls=%fused_computation.12.clone | custom fusion | bytes 6291488 | tf_op jit(solution)/shard_map/jit(_take)/gather | solution.py:68
  215.3 5.0 %gather_fusion.21 = bf16[8,768,256]{2,1,0:T(8,128)(2,1)} fusion(bf16[768,14,256]{2,0,1:T(8,128)(2,1)} %copy.46, s32[1024]{0:T(1024)S(1)} %pad_clamp_fusion.5), kind=kCustom, calls=%fused_computation.13.clone | custom fusion | bytes 6291488 | tf_op jit(solution)/shard_map/jit(_take)/gather | solution.py:68
  220.3 4.9 %gather_fusion.24 = bf16[8,768,256]{2,1,0:T(8,128)(2,1)} fusion(bf16[768,14,256]{2,0,1:T(8,128)(2,1)} %copy.46, s32[1024]{0:T(1024)S(1)} %pad_clamp_fusion.4), kind=kCustom, calls=%fused_computation.14.clone | custom fusion | bytes 6291488 | tf_op jit(solution)/shard_map/jit(_take)/gather | solution.py:68
  225.7 3.9 %fusion.181 = f32[8,256,32]{1,2,0:T(8,128)S(1)} fusion(bf16[8,768,256]{2,1,0:T(8,128)(2,1)} %gather_fusion.6, pred[8]{0:T(512)(128)(4,1)S(1)} %copy-done.8, f32[8,256]{1,0:T(8,128)S(1)} %add.371, f32[8,256]{1,0:T(8,128)S(1)} %broadcast_select_fusion.6, bf16[96,8,8,256]{3,2,1,0:T(8,128)(2,1)} %bitcast.278, bf16[8,32,256]{2,1,0:T(8,128)(2,1)S(1)} %gather_fusion.7, ...), kind=kOutput, calls=%fused_computation.117 | convolution fusion | flops 843186176 | bytes 6701072 | tf_op jit(solution)/shard_map/pia,iab->pib/dot_general | solution.py:73
  229.6 3.9 %fusion.176 = f32[8,256,32]{1,2,0:T(8,128)S(1)} fusion(f32[8,256,32]{1,2,0:T(8,128)S(1)} %fusion.181, bf16[8,768,256]{2,1,0:T(8,128)(2,1)} %gather_fusion.9, pred[8]{0:T(512)(128)(4,1)S(1)} %get-tuple-element.57, f32[8,256]{1,0:T(8,128)S(1)} %broadcast_select_fusion.5, f32[8,256]{1,0:T(8,128)S(1)} %add.371, bf16[96,8,8,256]{3,2,1,0:T(8,128)(2,1)} %bitcast.279, ...), kind=kOutput, calls=%fused_computation.116 | convolution fusion | flops 843251712 | bytes 6963216 | tf_op jit(solution)/shard_map/pia,iab->pib/dot_general | solution.py:73
  233.5 3.9 %fusion.166 = f32[8,256,32]{1,2,0:T(8,128)S(1)} fusion(f32[8,256,32]{1,2,0:T(8,128)S(1)} %fusion.176, bf16[8,768,256]{2,1,0:T(8,128)(2,1)} %gather_fusion.12, pred[8]{0:T(512)(128)(4,1)S(1)} %get-tuple-element.56, f32[8,256]{1,0:T(8,128)S(1)} %broadcast_select_fusion.4, f32[8,256]{1,0:T(8,128)S(1)} %add.371, bf16[96,8,8,256]{3,2,1,0:T(8,128)(2,1)} %bitcast.280, ...), kind=kOutput, calls=%fused_computation.114 | convolution fusion | flops 843251712 | bytes 6963216 | tf_op jit(solution)/shard_map/pia,iab->pib/dot_general | solution.py:73
  237.4 3.9 %fusion.156 = f32[8,256,32]{1,2,0:T(8,128)S(1)} fusion(f32[8,256,32]{1,2,0:T(8,128)S(1)} %fusion.166, bf16[8,768,256]{2,1,0:T(8,128)(2,1)} %gather_fusion.15, pred[8]{0:T(512)(128)(4,1)S(1)} %get-tuple-element.55, f32[8,256]{1,0:T(8,128)S(1)} %broadcast_select_fusion.3, f32[8,256]{1,0:T(8,128)S(1)} %add.371, bf16[96,8,8,256]{3,2,1,0:T(8,128)(2,1)} %bitcast.281, ...), kind=kOutput, calls=%fused_computation.112 | convolution fusion | flops 843251712 | bytes 6963216 | tf_op jit(solution)/shard_map/pia,iab->pib/dot_general | solution.py:73
  241.3 3.9 %fusion.146 = f32[8,256,32]{1,2,0:T(8,128)S(1)} fusion(f32[8,256,32]{1,2,0:T(8,128)S(1)} %fusion.156, bf16[8,768,256]{2,1,0:T(8,128)(2,1)} %gather_fusion.18, pred[8]{0:T(512)(128)(4,1)S(1)} %get-tuple-element.54, f32[8,256]{1,0:T(8,128)S(1)} %broadcast_select_fusion.2, f32[8,256]{1,0:T(8,128)S(1)} %add.371, bf16[96,8,8,256]{3,2,1,0:T(8,128)(2,1)} %bitcast.282, ...), kind=kOutput, calls=%fused_computation.110 | convolution fusion | flops 843251712 | bytes 6963216 | tf_op jit(solution)/shard_map/pia,iab->pib/dot_general | solution.py:73
  245.2 4.0 %fusion.136 = f32[8,256,32]{1,2,0:T(8,128)S(1)} fusion(f32[8,256,32]{1,2,0:T(8,128)S(1)} %fusion.146, bf16[8,768,256]{2,1,0:T(8,128)(2,1)} %gather_fusion.21, pred[8]{0:T(512)(128)(4,1)S(1)} %get-tuple-element.53, f32[8,256]{1,0:T(8,128)S(1)} %broadcast_select_fusion.1, f32[8,256]{1,0:T(8,128)S(1)} %add.371, bf16[96,8,8,256]{3,2,1,0:T(8,128)(2,1)} %bitcast.283, ...), kind=kOutput, calls=%fused_computation.108 | convolution fusion | flops 843251712 | bytes 6963216 | tf_op jit(solution)/shard_map/pia,iab->pib/dot_general | solution.py:73
  249.1 4.1 %fusion.126 = f32[8,4,8,256]{3,2,1,0:T(8,128)S(1)} fusion(f32[8,256,32]{1,2,0:T(8,128)S(1)} %fusion.136, bf16[8,768,256]{2,1,0:T(8,128)(2,1)} %gather_fusion.24, pred[8]{0:T(512)(128)(4,1)S(1)} %get-tuple-element.52, f32[8,256]{1,0:T(8,128)S(1)} %broadcast_select_fusion, f32[8,256]{1,0:T(8,128)S(1)} %add.371, bf16[96,8,8,256]{3,2,1,0:T(8,128)(2,1)} %bitcast.284, ...), kind=kOutput, calls=%fused_computation.106 | convolution fusion | flops 843251712 | bytes 6963216 | tf_op jit(solution)/shard_map/pia,iab->pib/dot_general | solution.py:73
  253.5 3.6 %reduce_sum.51 = f32[32,1920]{1,0:T(8,128)S(1)} reduce(f32[32,32,1920]{2,1,0:T(8,128)} %all-gather.4.cloned.1.call-done, f32[]{:T(128)} %constant.205.clone.1), dimensions={0}, to_apply=%region_3.7 | reduce | flops 1904640 | bytes 8110084 | tf_op jit(solution)/shard_map/reduce_sum | solution.py:136
  258.0 3.2 %fusion.44 = f32[2048,32]{0,1:T(8,128)S(1)} fusion(f32[32,2048]{1,0:T(8,128)S(1)} %bitcast.292, bf16[768,2048]{1,0:T(8,128)(2,1)} %param.13, f32[2048]{0:T(1024)S(1)} %multiply_reduce_fusion.1, f32[256]{0:T(256)S(1)} %multiply_reduce_fusion.2, bf16[768,64]{0,1:T(8,128)(2,1)S(1)} %get-tuple-element.28, bf16[768,64]{0,1:T(8,128)(2,1)S(1)} %get-tuple-element.30, ...), kind=kOutput, calls=%fused_computation.79 | convolution fusion | flops 843186176 | bytes 4088832 | tf_op jit(solution)/shard_map/dot_general | solution.py:150
  261.6 5.8 %scatter_custom_fusion = f32[32,2048]{0,1:T(8,128)S(1)} fusion(s32[2048]{0:T(1024)S(1)} %bitcast.294, f32[2048,32]{1,0:T(8,128)S(1)} %copy.80, f32[]{:T(128)} %constant.205.clone.1), kind=kCustom, calls=%fused_computation.168 | custom fusion | bytes 262148 | tf_op jit(solution)/shard_map/scatter | solution.py:154
  267.4 1.0 copy.81
  (86 shorter events, 7.0 us)
Async XLA Ops:
  6.5 250.6 %copy-start = (f32[30,64,64]{2,1,0:T(8,128)S(1)}, f32[30,64,64]{2,1,0:T(8,128)}, u32[]{:S(2)}) copy-start(f32[30,64,64]{2,1,0:T(8,128)} %param.19) | copy-start | bytes 1474564
  6.5 82.3 %all-gather.6.cloned.1.call-start = ((), (), s32[]{:S(2)}) async-start(), calls=%async_computation.1 | async-start | bytes 3244032 | tf_op jit(solution)/shard_map/all_gather | solution.py:103
  10.4 1.3 copy-start.6
  19.3 9.9 %copy-start.2 = (bf16[32,2048]{1,0:T(8,128)(2,1)S(1)}, bf16[32,2048]{1,0:T(8,128)(2,1)}, u32[]{:S(2)}) copy-start(bf16[32,2048]{1,0:T(8,128)(2,1)} %param.14) | copy-start | bytes 393220
  19.4 10.2 %copy-start.3 = (s32[1,2048]{1,0:T(1,128)S(1)}, s32[1,2048]{1,0:T(1,128)}, u32[]{:S(2)}) copy-start(s32[1,2048]{1,0:T(1,128)} %param.15) | copy-start | bytes 24580
  29.1 224.3 %all-gather.4.cloned.1.call-start = ((), (), s32[]{:S(2)}) async-start(), calls=%async_computation | async-start | bytes 8110080 | tf_op jit(solution)/shard_map/all_gather | solution.py:136
  113.0 0.7 copy-start.1
  116.6 9.9 %copy-start.4 = (s32[8]{0:T(128)S(1)}, s32[8]{0:T(128)}, u32[]{:S(2)}) copy-start(s32[8]{0:T(128)} %get-tuple-element.6) | copy-start | bytes 100
  116.6 9.9 %copy-start.5 = (s32[8]{0:T(128)S(1)}, s32[8]{0:T(128)}, u32[]{:S(2)}) copy-start(s32[8]{0:T(128)} %get-tuple-element.8) | copy-start | bytes 100
  116.6 10.0 %copy-start.7 = (s32[8]{0:T(128)S(1)}, s32[8]{0:T(128)}, u32[]{:S(2)}) copy-start(s32[8]{0:T(128)} %copy-done.6) | copy-start | bytes 100
  116.6 10.1 %copy-start.9 = (s32[1,8]{1,0:T(1,128)S(1)}, s32[1,8]{1,0:T(1,128)}, u32[]{:S(2)}) copy-start(s32[1,8]{1,0:T(1,128)} %param.17) | copy-start | bytes 100
  119.1 40.5 %collective-permute-start.1 = (bf16[800,768]{1,0:T(8,128)(2,1)}, bf16[800,768]{1,0:T(8,128)(2,1)}, u32[]{:S(2)}, u32[]{:S(2)}) collective-permute-start(bf16[800,768]{1,0:T(8,128)(2,1)} %copy.43), channel_id=1, source_target_pairs={{1,0},{2,1},{3,2},{4,3},{5,4},{6,5},{7,6},{8,7},{9,8},{10,9},{11,1... | collective-permute-start | bytes 3686408 | tf_op jit(solution)/shard_map/ppermute | solution.py:21
  122.8 38.6 %collective-permute-start = (bf16[800,768]{1,0:T(8,128)(2,1)}, bf16[800,768]{1,0:T(8,128)(2,1)}, u32[]{:S(2)}, u32[]{:S(2)}) collective-permute-start(bf16[800,768]{1,0:T(8,128)(2,1)} %copy.42), channel_id=1, source_target_pairs={{0,1},{1,2},{2,3},{3,4},{4,5},{5,6},{6,7},{7,8},{8,9},{9,10},{10,1... | collective-permute-start | bytes 3686408 | tf_op jit(solution)/shard_map/ppermute | solution.py:18
  220.3 5.3 %copy-start.8 = (pred[8]{0:T(512)(128)(4,1)S(1)}, pred[8]{0:T(512)(128)(4,1)}, u32[]{:S(2)}) copy-start(pred[8]{0:T(512)(128)(4,1)} %get-tuple-element.58) | copy-start | bytes 28
Sparse Core Ops, SparseCore 0:
  29.3 59.5 all-gather.5
  113.9 83.1 all-gather.3
